TPU v7x, 32 devices: a whole 2x2x4 slice. The times are simulated.
32 devices in a mesh: wide: 8 (over z, y), narrow: 4 (over x, core).
Axes of the slice: x: 2, y: 2, z: 4, core: 2. Of those that a mesh axis runs over, the one named last changes fastest.
Arguments:
- media_feats: bfloat16 [8, 2048, 1536], P('wide', 'narrow'), may hold values from -6 to 6
- latents: bfloat16 [8, 64, 1536], P('wide', 'narrow'), may hold values from -6 to 6
- frame_counts: int32 [8], P('wide'), may hold values from 1 to 8, as said below
- media_mask: int32 [8, 2048], P('wide'), may hold values 0 or 1
- time_embed: bfloat16 [8, 1536], replicated, may hold values from -3 to 3
- media_gain: float32 [1536], replicated, may hold values from 0.1 to 1.9
- media_bias: float32 [1536], replicated, may hold values from -1.75 to 1.75
- latent_gain: float32 [1536], replicated, may hold values from 0.1 to 1.9
- latent_bias: float32 [1536], replicated, may hold values from -1.75 to 1.75
- ffn_gain: float32 [1536], replicated, may hold values from 0.1 to 1.9
- ffn_bias: float32 [1536], replicated, may hold values from -1.75 to 1.75
- query_weight: bfloat16 [1536, 1536], P('wide', 'narrow'), may hold values from -0.3125 to 0.3125
- keyval_weight: bfloat16 [1536, 2, 1536], P('wide', None, 'narrow'), may hold values from -0.15625 to 0.15625
- output_weight: bfloat16 [1536, 1536], P('narrow', 'wide'), may hold values from -0.625 to 0.625
- up_weight: bfloat16 [1536, 6144], P(None, 'narrow'), may hold values from -0.15625 to 0.15625
- down_weight: bfloat16 [6144, 1536], P('narrow'), may hold values from -0.078125 to 0.078125
- cotangent: bfloat16 [8, 64, 1536], P('wide', 'narrow'), may hold values from -6 to 6
Outputs:
- out_latents: bfloat16 [8, 64, 1536], P('wide', 'narrow')
- grad_media: bfloat16 [8, 2048, 1536], P('wide', 'narrow')
- grad_latents: bfloat16 [8, 64, 1536], P('wide', 'narrow')
- grad_time_embed: float32 [8, 1536], P(None, ('wide', 'narrow'))
- grad_media_gain: float32 [1536], P(('wide', 'narrow'))
- grad_media_bias: float32 [1536], P(('wide', 'narrow'))
- grad_latent_gain: float32 [1536], P(('wide', 'narrow'))
- grad_latent_bias: float32 [1536], P(('wide', 'narrow'))
- grad_ffn_gain: float32 [1536], P(('wide', 'narrow'))
- grad_ffn_bias: float32 [1536], P(('wide', 'narrow'))
- grad_query_weight: float32 [1536, 1536], P('wide', 'narrow')
- grad_keyval_weight: float32 [1536, 2, 1536], P('wide', None, 'narrow')
- grad_output_weight: float32 [1536, 1536], P('narrow', 'wide')
- grad_up_weight: float32 [1536, 6144], P('wide', 'narrow')
- grad_down_weight: float32 [6144, 1536], P('narrow', 'wide')
Inputs may be any that keep to these rules, and one draw needn't show every extreme that they name: `frame_counts`: frames of each item; some item has exactly 8.
All inputs are finite; a program needn't handle non-finite values. No bound on the sum of `media_mask` on one device may be relied on, other than what follows from the above.
Results may differ from a plain program's by a relative error of at most 0.02.
Values may be sent and summed in bfloat16 or wider, within the bound.
A program may use at most 128 MiB of HBM per device.

v0:
```python
import math
import jax
import jax.numpy as jnp
from jax import lax
from jax.sharding import PartitionSpec as P

HEADS = 16
HEAD_DIM = 96
FRAMES_MAX = 8
PATCHES = 256
EPS = 1e-05
ENT_COEF = 4.0
HIGH = lax.Precision.HIGHEST


def norm_forward(values, norm_gain, norm_bias):
    row_mean = jnp.mean(values, axis=-1, keepdims=True)
    centered = values - row_mean
    inv_std = lax.rsqrt(jnp.mean(centered * centered, axis=-1, keepdims=True) + EPS)
    normed = centered * inv_std
    return (normed * norm_gain + norm_bias, normed, inv_std)


def norm_backward(grad_out, normed, inv_std, norm_gain):
    scaled = grad_out * norm_gain
    grad_in = inv_std * (
        scaled
        - jnp.mean(scaled, axis=-1, keepdims=True)
        - normed * jnp.mean(scaled * normed, axis=-1, keepdims=True)
    )
    return (grad_in, jnp.sum(grad_out * normed, axis=0), jnp.sum(grad_out, axis=0))


def gelu_slope(pre_act):
    cdf_part = 0.5 * (1.0 + lax.erf(pre_act * (1.0 / math.sqrt(2.0))))
    density = jnp.exp(-0.5 * pre_act * pre_act) * (1.0 / math.sqrt(2.0 * math.pi))
    return cdf_part + pre_act * density


def body(
    media_feats,
    latents,
    frame_counts,
    media_mask,
    time_embed,
    media_gain,
    media_bias,
    latent_gain,
    latent_bias,
    ffn_gain,
    ffn_bias,
    query_weight,
    keyval_weight,
    output_weight,
    up_weight,
    down_weight,
    cotangent,
):
    width = media_feats.shape[2]
    own_media = media_feats.shape[1]
    own_latent = latents.shape[1]
    narrow_size = lax.axis_size("narrow")
    wide_size = lax.axis_size("wide")
    narrow_pos = lax.axis_index("narrow")
    media_total = own_media * narrow_size
    latent_total = own_latent * narrow_size
    head_local = HEADS // narrow_size
    cols = head_local * HEAD_DIM
    key_total = media_total + latent_total
    f32, bf16 = (jnp.float32, jnp.bfloat16)

    def mm(spec, a, b):
        return jnp.einsum(spec, a, b, preferred_element_type=f32)

    all_ids = jnp.arange(media_total, dtype=jnp.int32) // PATCHES
    valid_one = (all_ids < frame_counts[0]) & (media_mask[0] > 0)
    local_count = jnp.sum(valid_one.astype(f32)) + float(latent_total)
    total_count = lax.psum(local_count, "wide")
    ent_weight = ENT_COEF * float(wide_size * media_total) / total_count
    kv_own = lax.all_gather(keyval_weight, "wide", axis=0, tiled=True).reshape(width, 2 * cols)
    query_own = lax.all_gather(query_weight, "wide", axis=0, tiled=True)
    output_own = lax.all_gather(output_weight, "wide", axis=1, tiled=True)
    own_ids = (narrow_pos * own_media + jnp.arange(own_media, dtype=jnp.int32)) // PATCHES
    frame_onehot = own_ids[:, None] == jnp.arange(FRAMES_MAX, dtype=jnp.int32)[None, :]
    time_rows = jnp.dot(frame_onehot.astype(bf16), time_embed, preferred_element_type=f32)
    score_scale = HEAD_DIM ** (-0.5)
    media_one, latent_one, cot_one = (media_feats[0], latents[0], cotangent[0])
    media_nf, media_hat, media_istd = norm_forward(
        media_one.astype(f32) + time_rows, media_gain, media_bias
    )
    latent_f32 = latent_one.astype(f32)
    latent_nf, latent_hat, latent_istd = norm_forward(latent_f32, latent_gain, latent_bias)
    latent_all = lax.all_gather(latent_nf.astype(bf16), "narrow", axis=0, tiled=True)
    cot_all = lax.all_gather(cot_one, "narrow", axis=0, tiled=True)
    media_all = lax.all_gather(media_nf.astype(bf16), "narrow", axis=0, tiled=True)
    keys_in = jnp.concatenate([media_all, latent_all], axis=0)
    query_act = mm("ld,dc->lc", latent_all, query_own).astype(bf16)
    key_vals = mm("kd,dc->kc", keys_in, kv_own).astype(bf16)
    query_heads = query_act.reshape(latent_total, head_local, HEAD_DIM)
    key_heads = key_vals[:, :cols].reshape(key_total, head_local, HEAD_DIM)
    value_heads = key_vals[:, cols:].reshape(key_total, head_local, HEAD_DIM)
    key_valid = jnp.concatenate([valid_one, jnp.ones((latent_total,), dtype=bool)])
    scores = mm("lhd,khd->hlk", query_heads, key_heads) * score_scale
    open_keys = key_valid[None, None, :]
    masked = jnp.where(open_keys, scores, -1e30)
    row_top = jnp.max(masked, axis=-1)
    expo = jnp.exp(masked - row_top[..., None])
    prob_all = expo / jnp.sum(expo, axis=-1)[..., None]
    prob_low = prob_all.astype(bf16)
    plain_scores = jnp.where(open_keys, scores, 0.0)
    mean_score = jnp.sum(prob_all * plain_scores, axis=-1)
    attn_out = mm("hlk,khd->lhd", prob_low, value_heads).reshape(latent_total, cols)
    attn_low = attn_out.astype(bf16)
    branch_part = mm("lc,cd->ld", attn_low, output_own)
    branch_own = lax.psum_scatter(
        branch_part.astype(bf16), "narrow", scatter_dimension=0, tiled=True
    ).astype(f32)
    latent_mid = latent_f32 + branch_own
    hidden_f, hidden_hat, hidden_istd = norm_forward(latent_mid, ffn_gain, ffn_bias)
    hidden_all = lax.all_gather(hidden_f.astype(bf16), "narrow", axis=0, tiled=True)
    pre_act = mm("ld,df->lf", hidden_all, up_weight)
    act_low = jax.nn.gelu(pre_act, approximate=False).astype(bf16)
    grad_act = mm("ld,fd->lf", cot_all, down_weight)
    grad_pre = (grad_act * gelu_slope(pre_act)).astype(bf16)
    hidden_part = mm("lf,df->ld", grad_pre, up_weight)
    grad_hidden = lax.psum_scatter(
        hidden_part.astype(bf16), "narrow", scatter_dimension=0, tiled=True
    ).astype(f32)
    grad_norm, fg_part, fb_part = norm_backward(grad_hidden, hidden_hat, hidden_istd, ffn_gain)
    grad_mid = cot_one.astype(f32) + grad_norm
    grad_branch_all = lax.all_gather(grad_mid.astype(bf16), "narrow", axis=0, tiled=True)
    ffn_part = mm("lf,fd->ld", act_low, down_weight)
    ffn_own = lax.psum_scatter(
        ffn_part.astype(bf16), "narrow", scatter_dimension=0, tiled=True
    ).astype(f32)
    out_one = (latent_mid + ffn_own).astype(bf16)
    grad_attn = mm("ld,cd->lc", grad_branch_all, output_own).astype(bf16)
    row_dots = jnp.sum(
        (grad_attn.astype(f32) * attn_out).reshape(latent_total, head_local, HEAD_DIM), axis=-1
    )
    shift_rows = (jnp.transpose(row_dots, (1, 0)) - ent_weight * mean_score)[..., None]
    grad_heads = grad_attn.reshape(latent_total, head_local, HEAD_DIM)
    grad_prob = mm("lhd,khd->hlk", grad_heads, value_heads)
    grad_scores = (prob_all * (grad_prob - ent_weight * plain_scores - shift_rows)).astype(bf16)
    grad_values = mm("hlk,lhd->khd", prob_low, grad_heads).reshape(key_total, cols)
    grad_keys = mm("hlk,lhd->khd", grad_scores, query_heads).reshape(key_total, cols) * score_scale
    grad_query = (
        mm("hlk,khd->lhd", grad_scores, key_heads).reshape(latent_total, cols) * score_scale
    ).astype(bf16)
    grad_pairs = jnp.concatenate([grad_keys, grad_values], axis=-1).astype(bf16)
    rows_part = mm("ke,de->kd", grad_pairs, kv_own)
    grad_media_rows = lax.psum_scatter(
        rows_part[:media_total].astype(bf16), "narrow", scatter_dimension=0, tiled=True
    ).astype(f32)
    latent_part = rows_part[media_total:] + mm("lc,dc->ld", grad_query, query_own)
    grad_latent_normed = lax.psum_scatter(
        latent_part.astype(bf16), "narrow", scatter_dimension=0, tiled=True
    ).astype(f32)
    keyval_grad = mm("kd,ke->de", keys_in, grad_pairs)
    keyval_sum = (
        lax.psum_scatter(keyval_grad.astype(bf16), "wide", scatter_dimension=0, tiled=True)
        .astype(f32)
        .reshape(width // wide_size, 2, cols)
    )
    tall = lax.all_gather(
        jnp.concatenate([act_low, grad_pre, attn_low, grad_query], axis=1),
        "wide",
        axis=0,
        tiled=True,
    )
    ff = up_weight.shape[1]
    act_g, pre_g, attn_g, query_g = (
        tall[:, :ff],
        tall[:, ff : 2 * ff],
        tall[:, 2 * ff : 2 * ff + cols],
        tall[:, 2 * ff + cols :],
    )
    cut = jnp.stack([latent_all, cot_all, hidden_all, grad_branch_all], axis=0)
    cut = cut.reshape(4, latent_total, wide_size, width // wide_size).transpose(2, 0, 1, 3)
    cut = lax.all_to_all(cut, "wide", split_axis=0, concat_axis=0, tiled=True)
    cut = cut.transpose(1, 0, 2, 3).reshape(4, wide_size * latent_total, width // wide_size)
    up_sum = mm("rd,rf->df", cut[2], pre_g)
    down_sum = mm("rf,rd->fd", act_g, cut[1])
    output_sum = mm("rc,rd->cd", attn_g, cut[3])
    query_sum = mm("rd,rc->dc", cut[0], query_g)
    grad_media_in, mg_part, mb_part = norm_backward(
        grad_media_rows, media_hat, media_istd, media_gain
    )
    time_part = jnp.einsum("mf,md->fd", frame_onehot.astype(f32), grad_media_in, precision=HIGH)
    grad_latent_in, lg_part, lb_part = norm_backward(
        grad_latent_normed, latent_hat, latent_istd, latent_gain
    )
    grad_latent_one = (grad_mid + grad_latent_in).astype(bf16)
    vectors = jnp.concatenate(
        [time_part, jnp.stack([mg_part, mb_part, lg_part, lb_part, fg_part, fb_part])], axis=0
    )
    vec = lax.psum_scatter(vectors, ("wide", "narrow"), scatter_dimension=1, tiled=True)
    return (
        out_one[None],
        grad_media_in.astype(bf16)[None],
        grad_latent_one[None],
        vec[:FRAMES_MAX],
        vec[FRAMES_MAX],
        vec[FRAMES_MAX + 1],
        vec[FRAMES_MAX + 2],
        vec[FRAMES_MAX + 3],
        vec[FRAMES_MAX + 4],
        vec[FRAMES_MAX + 5],
        query_sum,
        keyval_sum,
        output_sum,
        up_sum,
        down_sum,
    )


def solution(mesh):
    placed = (
        P("wide", "narrow", None),
        P("wide", "narrow", None),
        P("wide"),
        P("wide", None),
        P(),
        P(),
        P(),
        P(),
        P(),
        P(),
        P(),
        P("wide", "narrow"),
        P("wide", None, "narrow"),
        P("narrow", "wide"),
        P(None, "narrow"),
        P("narrow", None),
        P("wide", "narrow", None),
    )
    return jax.shard_map(
        body,
        mesh=mesh,
        in_specs=placed,
        out_specs=(
            P("wide", "narrow", None),
            P("wide", "narrow", None),
            P("wide", "narrow", None),
            P(None, ("wide", "narrow")),
            P(("wide", "narrow")),
            P(("wide", "narrow")),
            P(("wide", "narrow")),
            P(("wide", "narrow")),
            P(("wide", "narrow")),
            P(("wide", "narrow")),
            P("wide", "narrow"),
            P("wide", None, "narrow"),
            P("narrow", "wide"),
            P("wide", "narrow"),
            P("narrow", "wide"),
        ),
        check_vma=False,
    )
```

profile of v0, /device:TPU:0, one launch (start us, length us, event | category | flops | bytes accessed | tf_op | source)
XLA Modules:
  0.0 676.7 jit_solution(7399036223634174720)
XLA Ops:
  8.8 2.1 fusion.103
  11.6 1.7 add_convert_fusion
  15.6 6.9 %all_gather.28 = bf16[64,1536]{1,0:T(8,128)(2,1)S(1)} all-gather(bf16[16,1536]{1,0:T(8,128)(2,1)S(1)} %fusion.63), channel_id=1, replica_groups=mesh['wide'=8,'narrow'=4] {'narrow'}, dimensions={0}, use_global_device_ids=true | all-gather | bytes 245760 | tf_op jit(solution)/shard_map/all_gather | solution.py:93
  23.1 31.0 %all-gather.11.cloned.1.call-done = bf16[1536,384]{1,0:T(8,128)(2,1)} async-done(((bf16[192,384]{1,0:T(8,128)(2,1)}), bf16[1536,384]{1,0:T(8,128)(2,1)}) %all-gather.11.cloned.1.call-update) | async-done | bytes 1179664 | tf_op jit(solution)/shard_map/all_gather | solution.py:81
  54.1 1.6 convolution_convert_fusion.7
  55.8 51.0 %all-gather.9.cloned.1.call-done = bf16[1536,2,384]{2,1,0:T(2,128)(2,1)} async-done(((bf16[192,2,384]{2,1,0:T(2,128)(2,1)}), bf16[1536,2,384]{2,1,0:T(2,128)(2,1)}) %all-gather.9.cloned.1.call-update) | async-done | bytes 2359312 | tf_op jit(solution)/shard_map/all_gather | solution.py:80
  106.8 3.6 copy.106
  110.4 43.4 %all-gather.7.cloned.1.call-done = bf16[2048,1536]{1,0:T(8,128)(2,1)} async-done(((bf16[512,1536]{1,0:T(8,128)(2,1)}), bf16[2048,1536]{1,0:T(8,128)(2,1)}) %all-gather.7.cloned.1.call-update) | async-done | bytes 6291472 | tf_op jit(solution)/shard_map/all_gather | solution.py:95
  153.8 3.3 constant_dynamic-update-slice_fusion.1
  157.3 5.4 convolution_convert_fusion
  162.7 2.1 fusion.100
  164.8 3.8 copy.88
  168.6 3.8 copy.87
  172.3 3.7 fusion.104
  176.0 2.9 convolution_bitcast_fusion
  179.7 1.0 reshape.185
  181.4 15.6 %all-gather.13.cloned.1.call-done = bf16[384,1536]{0,1:T(8,128)(2,1)} async-done(((bf16[384,192]{0,1:T(8,128)(2,1)}), bf16[384,1536]{0,1:T(8,128)(2,1)}) %all-gather.13.cloned.1.call-update) | async-done | bytes 1179664 | tf_op jit(solution)/shard_map/all_gather | solution.py:82
  197.0 2.5 convolution_convert_fusion.5
  200.2 19.6 %psum.7 = f32[]{:T(128)} all-reduce(f32[]{:T(128)S(6)} %add.128), channel_id=1, replica_groups=mesh['wide'=8,'narrow'=4] {'wide'}, use_global_device_ids=true, to_apply=%region_14.15 | all-reduce | flops 1 | bytes 8 | tf_op jit(solution)/shard_map/psum | solution.py:78
  220.5 7.1 %all-gather = bf16[1,64,1536]{2,1,0:T(8,128)(2,1)} all-gather(bf16[1,16,1536]{2,1,0:T(8,128)(2,1)} %param.33), channel_id=2, replica_groups=mesh['wide'=8,'narrow'=4] {'narrow'}, dimensions={1}, use_global_device_ids=true | all-gather | bytes 245760 | tf_op jit(solution)/shard_map/all_gather | solution.py:94
  230.5 5.6 all_gather.32
  236.1 4.7 fusion.30
  240.8 3.9 fusion.14
  245.4 4.6 convolution_convert_fusion.3
  250.2 4.7 multiply_reduce_fusion.1
  254.9 11.4 %reduce-scatter.14.cloned.1.call-done = bf16[16,1536]{1,0:T(8,128)(2,1)} async-done(((bf16[64,1536]{1,0:T(8,128)(2,1)}), bf16[16,1536]{1,0:T(8,128)(2,1)}) %reduce-scatter.14.cloned.1.call-update) | async-done | bytes 49168 | tf_op jit(solution)/shard_map/reduce_scatter | solution.py:126
  266.3 1.5 fusion.74
  268.7 5.6 all_gather.34
  275.0 2.2 convert_multiply_fusion.6
  277.3 1.7 reshape.187
  278.9 1.0 reduce_sum.208
  281.4 3.6 convolution_convert_fusion.1
  287.4 1.8 fusion.7
  290.9 8.3 %fusion.16 = f32[2112,1536]{1,0:T(8,128)S(1)} fusion(bf16[1536,768]{1,0:T(8,128)(2,1)} %bitcast.147, bf16[2112,384]{0,1:T(8,128)(2,1)} %bitcast.166, bf16[2112,384]{0,1:T(8,128)(2,1)} %bitcast.152), kind=kOutput, calls=%fused_computation.37 | convolution fusion | flops 4989321216 | bytes 18579456 | tf_op jit(solution)/shard_map/ke,de->kd/dot_general | solution.py:73
  299.3 4.6 copy-done.7
  303.9 1.2 fusion.15
  305.1 4.1 convolution_convert_fusion.4
  309.5 10.1 %convolution_convert_fusion.2 = bf16[1536,768]{1,0:T(8,128)(2,1)} fusion(bf16[2112,1536]{1,0:T(8,128)(2,1)} %copy-done.4, bf16[2112,384]{0,1:T(8,128)(2,1)} %bitcast.167, bf16[2112,384]{0,1:T(8,128)(2,1)} %bitcast.153), kind=kOutput, calls=%fused_computation.19 | convolution fusion | flops 4990500864 | bytes 12091392 | tf_op jit(solution)/shard_map/kd,ke->de/dot_general | solution.py:73
  320.4 1.9 pad_maximum_fusion.3
  322.3 8.0 %slice.110 = bf16[2048,1536]{1,0:T(8,128)(2,1)} slice(f32[2112,1536]{1,0:T(8,128)} %copy-done.7), slice={[0:2048], [0:1536]} | slice | bytes 12582912 | tf_op jit(solution)/shard_map/slice | solution.py:153
  330.3 1.9 stack.40
  333.1 1.9 stack.41
  335.0 1.9 stack.42
  336.9 1.4 maximum_bitcast_fusion
  338.4 1.2 copy.96
  339.6 5.5 all-to-all-start
  347.3 1.6 fusion.84
  348.9 33.9 %all-to-all-done = bf16[8,4,64,192]{3,2,1,0:T(8,128)(2,1)} async-done(((bf16[8,4,64,192]{3,2,1,0:T(8,128)(2,1)}), bf16[8,4,64,192]{3,2,1,0:T(8,128)(2,1)}, u32[]{:S(2)}, u32[]{:S(2)}) %all-to-all-start) | async-done | bytes 786464 | tf_op jit(solution)/shard_map/all_to_all | solution.py:180
  382.8 2.1 fusion.101
  384.9 43.5 %reduce-scatter.20.cloned.1.call-done = bf16[192,768]{1,0:T(8,128)(2,1)} async-done(((bf16[1536,768]{1,0:T(8,128)(2,1)}), bf16[192,768]{1,0:T(8,128)(2,1)}) %reduce-scatter.20.cloned.1.call-update) | async-done | bytes 294928 | tf_op jit(solution)/shard_map/reduce_scatter | solution.py:161
  428.4 2.1 reshape.193
  430.5 69.3 %all-gather.15.cloned.1.call-done = bf16[512,3840]{1,0:T(8,128)(2,1)} async-done(((bf16[64,3840]{1,0:T(8,128)(2,1)}), bf16[512,3840]{1,0:T(8,128)(2,1)}) %all-gather.15.cloned.1.call-update) | async-done | bytes 3932176 | tf_op jit(solution)/shard_map/all_gather | solution.py:165
  499.7 2.1 fusion.35
  501.8 3.0 fusion.18
  504.8 3.0 fusion.20
  507.8 52.1 %reduce-scatter.16.cloned.1.call-done = bf16[512,1536]{1,0:T(8,128)(2,1)} async-done(((bf16[2048,1536]{1,0:T(8,128)(2,1)}), bf16[512,1536]{1,0:T(8,128)(2,1)}) %reduce-scatter.16.cloned.1.call-update) | async-done | bytes 1572880 | tf_op jit(solution)/shard_map/reduce_scatter | solution.py:152
  559.8 2.9 fusion.13
  562.8 2.1 convert_bitcast_fusion
  565.0 1.2 fusion.46
  566.2 1.2 copy.97
  567.5 2.0 fusion.37
  569.5 94.4 %reduce-scatter.22.cloned.1.call-done = f32[48,14]{1,0:T(8,128)} async-done(((f32[1536,14]{1,0:T(8,128)}), f32[48,14]{1,0:T(8,128)}) %reduce-scatter.22.cloned.1.call-update) | async-done | bytes 2704
  663.9 1.1 fusion.102
  665.0 1.4 copy.99
  (187 shorter events, 24.6 us)
Async XLA Ops:
  7.2 1.6 copy-start
  7.2 46.9 %all-gather.11.cloned.1.call-start = ((), (), s32[]{:S(2)}) async-start(), calls=%async_computation.10 | async-start | bytes 1327104 | tf_op jit(solution)/shard_map/all_gather | solution.py:81
  7.9 98.9 %all-gather.9.cloned.1.call-start = ((), (), s32[]{:S(2)}) async-start(), calls=%async_computation.9 | async-start | bytes 2654208 | tf_op jit(solution)/shard_map/all_gather | solution.py:80
  8.7 145.2 %all-gather.7.cloned.1.call-start = ((), (), s32[]{:S(2)}) async-start(), calls=%async_computation.8 | async-start | bytes 7864320 | tf_op jit(solution)/shard_map/all_gather | solution.py:95
  8.8 2.1 copy-start.30
  11.6 3.0 copy-start.5
  11.6 3.4 copy-start.41
  11.6 3.9 copy-start.26
  11.6 3.9 copy-start.39
  13.4 183.7 %all-gather.13.cloned.1.call-start = ((), (), s32[]{:S(2)}) async-start(), calls=%async_computation.11 | async-start | bytes 1327104 | tf_op jit(solution)/shard_map/all_gather | solution.py:82
  13.9 213.7 %reduce-scatter.10.cloned.1.call-start = ((), (), s32[]{:S(2)}) async-start(), calls=%async_computation.12 | async-start | bytes 245760 | tf_op jit(solution)/shard_map/reduce_scatter | solution.py:115
  14.8 95.6 %copy-start.35 = (f32[16]{0:T(128)}, f32[16]{0:T(128)S(1)}, u32[]{:S(2)}) copy-start(f32[16]{0:T(128)S(1)} %broadcast_multiply_fusion.8) | copy-start | bytes 196
  23.1 227.1 %copy-start.49 = (pred[2112]{0:T(1024)(128)(4,1)}, pred[2112]{0:T(1024)(128)(4,1)S(1)}, u32[]{:S(2)}) copy-start(pred[2112]{0:T(1024)(128)(4,1)S(1)} %concatenate.18) | copy-start | bytes 6340
  55.8 116.6 %copy-start.22 = (bf16[64,4,96]{2,1,0:T(4,128)(2,1)}, bf16[64,4,96]{2,1,0:T(4,128)(2,1)S(1)}, u32[]{:S(2)}) copy-start(bf16[64,4,96]{2,1,0:T(4,128)(2,1)S(1)} %reshape.183) | copy-start | bytes 147460
  153.8 3.5 copy-start.8
  157.2 5.5 copy-start.4
  176.0 74.2 %copy-start.54 = (f32[4,64]{1,0:T(4,128)}, f32[4,64]{1,0:T(4,128)S(1)}, u32[]{:S(2)}) copy-start(f32[4,64]{1,0:T(4,128)S(1)} %get-tuple-element.47) | copy-start | bytes 3076
  179.0 50.6 %copy-start.24 = (f32[1536]{0:T(1024)S(1)}, f32[1536]{0:T(1024)}, u32[]{:S(2)}) copy-start(f32[1536]{0:T(1024)} %param.26) | copy-start | bytes 18436
  179.0 50.6 %copy-start.40 = (f32[1536]{0:T(1024)S(1)}, f32[1536]{0:T(1024)}, u32[]{:S(2)}) copy-start(f32[1536]{0:T(1024)} %param.27) | copy-start | bytes 18436
  180.8 60.0 %copy-start.15 = (f32[64,384]{1,0:T(8,128)}, f32[64,384]{1,0:T(8,128)S(1)}, u32[]{:S(2)}) copy-start(f32[64,384]{1,0:T(8,128)S(1)} %reshape.185) | copy-start | bytes 294916
  199.5 66.8 %reduce-scatter.14.cloned.1.call-start = ((), (), s32[]{:S(2)}) async-start(), calls=%async_computation.14 | async-start | bytes 245760 | tf_op jit(solution)/shard_map/reduce_scatter | solution.py:126
  228.6 39.2 %copy-start.32 = (f32[16]{0:T(128)}, f32[16]{0:T(128)S(1)}, u32[]{:S(2)}) copy-start(f32[16]{0:T(128)S(1)} %broadcast_multiply_fusion.7) | copy-start | bytes 196
  229.6 38.2 %copy-start.37 = (f32[16]{0:T(128)}, f32[16]{0:T(128)S(1)}, u32[]{:S(2)}) copy-start(f32[16]{0:T(128)S(1)} %add_rsqrt_fusion.1) | copy-start | bytes 196
  236.1 4.7 copy-start.16
  236.1 4.7 copy-start.10
  250.0 16.3 %copy-start.12 = (bf16[16,1536]{1,0:T(8,128)(2,1)S(1)}, bf16[16,1536]{1,0:T(8,128)(2,1)}, u32[]{:S(2)}) copy-start(bf16[16,1536]{1,0:T(8,128)(2,1)} %reduce-scatter.10.cloned.1.call-done) | copy-start | bytes 147460
  250.0 17.9 %copy-start.19 = (bf16[1,16,1536]{2,1,0:T(8,128)(2,1)S(1)}, bf16[1,16,1536]{2,1,0:T(8,128)(2,1)}, u32[]{:S(2)}) copy-start(bf16[1,16,1536]{2,1,0:T(8,128)(2,1)} %param.33) | copy-start | bytes 147460
  250.0 95.3 %reduce-scatter.18.cloned.1.call-start = ((), (), s32[]{:S(2)}) async-start(), calls=%async_computation.16 | async-start | bytes 245760 | tf_op jit(solution)/shard_map/reduce_scatter | solution.py:156
  267.8 9.5 %copy-start.45 = (f32[16]{0:T(128)}, f32[16]{0:T(128)S(1)}, u32[]{:S(2)}) copy-start(f32[16]{0:T(128)S(1)} %get-tuple-element.55) | copy-start | bytes 196
  267.8 9.5 %copy-start.47 = (f32[16]{0:T(128)}, f32[16]{0:T(128)S(1)}, u32[]{:S(2)}) copy-start(f32[16]{0:T(128)S(1)} %get-tuple-element.56) | copy-start | bytes 196
  281.4 3.7 copy-start.42
  281.4 3.7 copy-start.51
  281.4 3.7 copy-start.13
  281.4 3.7 copy-start.27
  281.4 3.7 copy-start.50
  281.4 3.7 copy-start.52
  281.4 3.7 copy-start.53
  281.4 3.7 copy-start.55
  285.1 1.4 copy-start.2
  286.6 0.8 copy-start.23
  290.9 8.4 %copy-start.21 = (bf16[64,384]{1,0:T(8,128)(2,1)}, bf16[64,384]{1,0:T(8,128)(2,1)S(1)}, u32[]{:S(2)}) copy-start(bf16[64,384]{1,0:T(8,128)(2,1)S(1)} %convert_element_type.140) | copy-start | bytes 147460
  290.9 13.0 %copy-start.6 = (bf16[1536,384]{1,0:T(8,128)(2,1)S(1)}, bf16[1536,384]{1,0:T(8,128)(2,1)}, u32[]{:S(2)}) copy-start(bf16[1536,384]{1,0:T(8,128)(2,1)} %all-gather.11.cloned.1.call-done) | copy-start | bytes 3538948
  299.3 4.6 copy-start.7
  305.1 42.2 %reduce-scatter.12.cloned.1.call-start = ((), (), s32[]{:S(2)}) async-start(), calls=%async_computation.13 | async-start | bytes 245760 | tf_op jit(solution)/shard_map/reduce_scatter | solution.py:133
  309.2 119.2 %reduce-scatter.20.cloned.1.call-start = ((), (), s32[]{:S(2)}) async-start(), calls=%async_computation.18 | async-start | bytes 2654208 | tf_op jit(solution)/shard_map/reduce_scatter | solution.py:161
  319.6 0.8 copy-start.17
  319.6 180.1 %all-gather.15.cloned.1.call-start = ((), (), s32[]{:S(2)}) async-start(), calls=%async_computation.17 | async-start | bytes 4423680 | tf_op jit(solution)/shard_map/all_gather | solution.py:165
  322.3 237.5 %reduce-scatter.16.cloned.1.call-start = ((), (), s32[]{:S(2)}) async-start(), calls=%async_computation.15 | async-start | bytes 7864320 | tf_op jit(solution)/shard_map/reduce_scatter | solution.py:152
  338.3 6.9 %copy-start.29 = (f32[1536]{0:T(1024)S(1)}, f32[1536]{0:T(1024)}, u32[]{:S(2)}) copy-start(f32[1536]{0:T(1024)} %get-tuple-element.19) | copy-start | bytes 18436
  338.3 6.9 %copy-start.28 = (f32[1536]{0:T(1024)S(1)}, f32[1536]{0:T(1024)}, u32[]{:S(2)}) copy-start(f32[1536]{0:T(1024)} %get-tuple-element.25) | copy-start | bytes 18436
  338.3 7.0 %copy-start.36 = (f32[16]{0:T(128)S(1)}, f32[16]{0:T(128)}, u32[]{:S(2)}) copy-start(f32[16]{0:T(128)} %copy-done.35) | copy-start | bytes 196
  338.4 7.0 %copy-start.44 = (f32[16]{0:T(128)S(1)}, f32[16]{0:T(128)}, u32[]{:S(2)}) copy-start(f32[16]{0:T(128)} %copy-done.43) | copy-start | bytes 196
  338.4 8.9 %copy-start.18 = (bf16[16,1536]{1,0:T(8,128)(2,1)S(1)}, bf16[16,1536]{1,0:T(8,128)(2,1)}, u32[]{:S(2)}) copy-start(bf16[16,1536]{1,0:T(8,128)(2,1)} %reduce-scatter.14.cloned.1.call-done) | copy-start | bytes 147460
  338.4 8.9 %copy-start.20 = (bf16[1,16,1536]{2,1,0:T(8,128)(2,1)S(1)}, bf16[1,16,1536]{2,1,0:T(8,128)(2,1)}, u32[]{:S(2)}) copy-start(bf16[1,16,1536]{2,1,0:T(8,128)(2,1)} %param.33) | copy-start | bytes 147460
  338.4 8.9 %copy-start.33 = (f32[16]{0:T(128)S(1)}, f32[16]{0:T(128)}, u32[]{:S(2)}) copy-start(f32[16]{0:T(128)} %copy-done.32) | copy-start | bytes 196
  338.4 8.9 %copy-start.38 = (f32[16]{0:T(128)S(1)}, f32[16]{0:T(128)}, u32[]{:S(2)}) copy-start(f32[16]{0:T(128)} %copy-done.37) | copy-start | bytes 196
  338.4 8.9 %copy-start.46 = (f32[16]{0:T(128)S(1)}, f32[16]{0:T(128)}, u32[]{:S(2)}) copy-start(f32[16]{0:T(128)} %copy-done.45) | copy-start | bytes 196
  338.4 8.9 %copy-start.48 = (f32[16]{0:T(128)S(1)}, f32[16]{0:T(128)}, u32[]{:S(2)}) copy-start(f32[16]{0:T(128)} %copy-done.47) | copy-start | bytes 196
  339.6 43.1 %all-to-all-start = ((bf16[8,4,64,192]{3,2,1,0:T(8,128)(2,1)}), bf16[8,4,64,192]{3,2,1,0:T(8,128)(2,1)}, u32[]{:S(2)}, u32[]{:S(2)}) async-start(bf16[8,4,64,192]{3,2,1,0:T(8,128)(2,1)} %copy.96), calls=%async_computation.5 | async-start | bytes 2097152 | tf_op jit(solution)/shard_map/all_to_all | solution.py:180
  345.2 318.7 %reduce-scatter.22.cloned.1.call-start = ((), (), s32[]{:S(2)}) async-start(), calls=%async_computation.19 | async-start | bytes 811008
  559.8 3.0 copy-start.3
  562.8 2.2 copy-start.31
  565.0 2.5 copy-start.14
  565.0 104.9 %copy-start.1 = (bf16[8,1536]{1,0:T(8,128)(2,1)S(1)}, bf16[8,1536]{1,0:T(8,128)(2,1)}, u32[]{:S(2)}) copy-start(bf16[8,1536]{1,0:T(8,128)(2,1)} %param.21) | copy-start | bytes 73732
  (5 other events, 3.3 us)
Sparse Core Ops, SparseCore 0:
  10.2 43.8 all-gather.10
  56.2 50.4 all-gather.8
  108.9 44.8 all-gather.6
  155.9 41.1 all-gather.12
  199.9 18.4 reduce-scatter.9
  250.1 16.1 reduce-scatter.13
  305.2 19.7 reduce-scatter.17
  327.5 19.7 reduce-scatter.11
  350.8 77.5 reduce-scatter.19
  431.0 68.6 all-gather.14
  502.3 57.4 reduce-scatter.15
  567.6 96.2 reduce-scatter.21
where the time goes:
time: 679 us; the launch traced here: 677 us
  waiting for transfers between devices  449 us (66%)
  matrix products  79.9 us (12%)
  local copies, waits for them, and re-layouts  58.9 us (9%)
  blocking collectives  44.8 us (7%)
  other arithmetic  21.2 us (3%)
  between operations  16.9 us (2%)
    unnamed x13, waiting for transfers between devices  96.5 us
    dot_general x21, matrix products, mm(): return jnp.einsum(spec, a, b, preferred_element_type=f32)  73 us
    all_gather x1, waiting for transfers between devices, body(): lax.all_gather(jnp.concatenate([act_low, grad_pre, attn_low, grad_query],...  69.3 us
    reduce_scatter x1, waiting for transfers between devices, body(): lax.psum_scatter(rows_part[:media_total].astype(bf16), 'narrow', scatter_...  52.1 us
    all_gather x1, waiting for transfers between devices, body(): lax.all_gather(keyval_weight, 'wide', axis=0, tiled=True)  51 us
    reduce_scatter x1, waiting for transfers between devices, body(): lax.psum_scatter(keyval_grad.astype(bf16), 'wide', scatter_dimension=0, t...  43.5 us
    all_gather x1, waiting for transfers between devices, body(): lax.all_gather(media_nf.astype(bf16), 'narrow', axis=0, tiled=True)  43.4 us
    all_to_all x1, waiting for transfers between devices, body(): cut = lax.all_to_all(cut, 'wide', split_axis=0, concat_axis=0, tiled=True)  33.9 us
  transfers between devices with their start and end apart: 13, of which 11 were waited for; matrix products, arithmetic and copies ran while one was open for 14% of the time, Pallas kernels for 0%

commit v1 on v0

--- a/solution.py
+++ b/solution.py
@@ -162,12 +162,15 @@
         .astype(f32)
         .reshape(width // wide_size, 2, cols)
     )
-    tall = lax.all_gather(
-        jnp.concatenate([act_low, grad_pre, attn_low, grad_query], axis=1),
-        "wide",
-        axis=0,
-        tiled=True,
-    )
+    x = jnp.concatenate([act_low, grad_pre, attn_low, grad_query], axis=1)
+    ways = lax.axis_size("wide")
+    pieces = [x]
+    for far in range(1, ways):
+        pieces.append(
+            lax.ppermute(pieces[far - 1], "wide", [(d, (d - 1) % ways) for d in range(ways)])
+        )
+    line = jnp.concatenate(pieces, axis=0)
+    tall = jnp.roll(line, lax.axis_index("wide") * x.shape[0], axis=0)
     ff = up_weight.shape[1]
     act_g, pre_g, attn_g, query_g = (
         tall[:, :ff],

time: 679 us -> 611 us (0.90)
  waiting for transfers between devices: 449 us -> 325 us
  starting transfers between devices: 6.41 us -> 39.6 us
  local copies, waits for them, and re-layouts: 58.9 us -> 80 us
    all_gather x1 -> x0, waiting for transfers between devices: 69.3 us -> none  [body(): lax.all_gather(jnp.concatenate([act_low, grad_pre, attn_low, grad_query],...]
    ppermute x0 -> x7, waiting for transfers between devices: none -> 62.1 us  [body(): lax.ppermute(pieces[far - 1], 'wide', [(d, (d - 1) % ways) for d in range...]
    reduce_scatter x1, waiting for transfers between devices: 52.1 us -> 0.01 us  [body(): lax.psum_scatter(rows_part[:media_total].astype(bf16), 'narrow', scatter_...]
    reduce_scatter x1, waiting for transfers between devices: 43.5 us -> 7.32 us  [body(): lax.psum_scatter(keyval_grad.astype(bf16), 'wide', scatter_dimension=0, t...]
    ppermute x0 -> x7, starting transfers between devices: none -> 34.7 us  [body(): lax.ppermute(pieces[far - 1], 'wide', [(d, (d - 1) % ways) for d in range...]
    all_to_all x1, waiting for transfers between devices: 33.9 us -> 0.01 us  [body(): cut = lax.all_to_all(cut, 'wide', split_axis=0, concat_axis=0, tiled=True)]
    unnamed x122 -> x119, local copies, waits for them, and re-layouts: 21.7 us -> 40.9 us
    unnamed x13 -> x12, waiting for transfers between devices: 96.5 us -> 101 us
  transfers between devices with their start and end apart: 13 -> 19, of which waited for: 11 -> 13; matrix products, arithmetic and copies ran while one was open for 14% -> 20% of each run, Pallas kernels for 0% -> 0%
where the time goes in v1:
time: 611 us; the launch traced here: 608 us
  waiting for transfers between devices  325 us (53%)
  local copies, waits for them, and re-layouts  80 us (13%)
  matrix products  79.6 us (13%)
  blocking collectives  44.8 us (7%)
  starting transfers between devices  39.6 us (6%)
  other arithmetic  22.7 us (4%)
  between operations  16.5 us (3%)
    unnamed x12, waiting for transfers between devices  101 us
    dot_general x21, matrix products, mm(): return jnp.einsum(spec, a, b, preferred_element_type=f32)  72.6 us
    ppermute x7, waiting for transfers between devices, body(): lax.ppermute(pieces[far - 1], 'wide', [(d, (d - 1) % ways) for d in range...  62.1 us
    all_gather x1, waiting for transfers between devices, body(): lax.all_gather(keyval_weight, 'wide', axis=0, tiled=True)  51 us
    all_gather x1, waiting for transfers between devices, body(): lax.all_gather(media_nf.astype(bf16), 'narrow', axis=0, tiled=True)  43.4 us
    unnamed x119, local copies, waits for them, and re-layouts  40.9 us
    ppermute x7, starting transfers between devices, body(): lax.ppermute(pieces[far - 1], 'wide', [(d, (d - 1) % ways) for d in range...  34.7 us
    all_gather x1, waiting for transfers between devices, body(): query_own = lax.all_gather(query_weight, 'wide', axis=0, tiled=True)  31.1 us
  transfers between devices with their start and end apart: 19, of which 13 were waited for; matrix products, arithmetic and copies ran while one was open for 20% of the time, Pallas kernels for 0%

profile of v1, /device:TPU:0, one launch (start us, length us, event | category | flops | bytes accessed | tf_op | source)
XLA Modules:
  0.0 608.5 jit_solution(10456434387805269405)
XLA Ops:
  8.8 2.1 fusion.104
  15.4 6.9 %all_gather.25 = bf16[64,1536]{1,0:T(8,128)(2,1)S(1)} all-gather(bf16[16,1536]{1,0:T(8,128)(2,1)S(1)} %fusion.63), channel_id=1, replica_groups=mesh['wide'=8,'narrow'=4] {'narrow'}, dimensions={0}, use_global_device_ids=true | all-gather | bytes 245760 | tf_op jit(solution)/shard_map/all_gather | solution.py:93
  22.9 31.1 %all-gather.10.cloned.1.call-done = bf16[1536,384]{1,0:T(8,128)(2,1)} async-done(((bf16[192,384]{1,0:T(8,128)(2,1)}), bf16[1536,384]{1,0:T(8,128)(2,1)}) %all-gather.10.cloned.1.call-update) | async-done | bytes 1179664 | tf_op jit(solution)/shard_map/all_gather | solution.py:81
  55.8 51.0 %all-gather.8.cloned.1.call-done = bf16[1536,2,384]{2,1,0:T(2,128)(2,1)} async-done(((bf16[192,2,384]{2,1,0:T(2,128)(2,1)}), bf16[1536,2,384]{2,1,0:T(2,128)(2,1)}) %all-gather.8.cloned.1.call-update) | async-done | bytes 2359312 | tf_op jit(solution)/shard_map/all_gather | solution.py:80
  106.8 3.6 copy.106
  110.4 43.4 %all-gather.6.cloned.1.call-done = bf16[2048,1536]{1,0:T(8,128)(2,1)} async-done(((bf16[512,1536]{1,0:T(8,128)(2,1)}), bf16[2048,1536]{1,0:T(8,128)(2,1)}) %all-gather.6.cloned.1.call-update) | async-done | bytes 6291472 | tf_op jit(solution)/shard_map/all_gather | solution.py:95
  153.8 3.3 constant_dynamic-update-slice_fusion.1
  157.3 5.4 convolution_convert_fusion
  162.7 2.0 fusion.101
  164.8 3.8 copy.88
  168.5 3.8 copy.87
  172.3 3.7 fusion.105
  176.0 2.9 convolution_bitcast_fusion
  179.2 17.8 %all-gather.12.cloned.1.call-done = bf16[384,1536]{0,1:T(8,128)(2,1)} async-done(((bf16[384,192]{0,1:T(8,128)(2,1)}), bf16[384,1536]{0,1:T(8,128)(2,1)}) %all-gather.12.cloned.1.call-update) | async-done | bytes 1179664 | tf_op jit(solution)/shard_map/all_gather | solution.py:82
  197.0 2.4 convolution_convert_fusion.5
  200.2 19.6 %psum.7 = f32[]{:T(128)} all-reduce(f32[]{:T(128)S(6)} %add.138), channel_id=1, replica_groups=mesh['wide'=8,'narrow'=4] {'wide'}, use_global_device_ids=true, to_apply=%region_14.15 | all-reduce | flops 1 | bytes 8 | tf_op jit(solution)/shard_map/psum | solution.py:78
  220.5 7.1 %all-gather = bf16[1,64,1536]{2,1,0:T(8,128)(2,1)} all-gather(bf16[1,16,1536]{2,1,0:T(8,128)(2,1)} %param.33), channel_id=2, replica_groups=mesh['wide'=8,'narrow'=4] {'narrow'}, dimensions={1}, use_global_device_ids=true | all-gather | bytes 245760 | tf_op jit(solution)/shard_map/all_gather | solution.py:94
  230.5 5.6 all_gather.29
  236.1 4.7 fusion.30
  240.8 3.9 fusion.14
  244.7 4.5 convolution_convert_fusion.3
  249.5 4.7 multiply_reduce_fusion.1
  254.2 11.4 %reduce-scatter.14.cloned.1.call-done = bf16[16,1536]{1,0:T(8,128)(2,1)} async-done(((bf16[64,1536]{1,0:T(8,128)(2,1)}), bf16[16,1536]{1,0:T(8,128)(2,1)}) %reduce-scatter.14.cloned.1.call-update) | async-done | bytes 49168 | tf_op jit(solution)/shard_map/reduce_scatter | solution.py:126
  268.1 5.6 all_gather.31
  274.3 2.3 convert_multiply_fusion.6
  281.5 3.6 convolution_convert_fusion.1
  291.5 8.3 %fusion.16 = f32[2112,1536]{1,0:T(8,128)S(1)} fusion(bf16[1536,768]{1,0:T(8,128)(2,1)} %bitcast.147, bf16[2112,384]{0,1:T(8,128)(2,1)} %bitcast.166, bf16[2112,384]{0,1:T(8,128)(2,1)} %bitcast.150), kind=kOutput, calls=%fused_computation.37 | convolution fusion | flops 4989321216 | bytes 18579456 | tf_op jit(solution)/shard_map/ke,de->kd/dot_general | solution.py:73
  299.8 4.6 copy-done.7
  305.7 4.1 convolution_convert_fusion.4
  309.8 8.1 %slice.98 = bf16[2048,1536]{1,0:T(8,128)(2,1)} slice(f32[2112,1536]{1,0:T(8,128)} %copy-done.7), slice={[0:2048], [0:1536]} | slice | bytes 12582912 | tf_op jit(solution)/shard_map/slice | solution.py:153
  318.0 2.0 pad_maximum_fusion.3
  320.0 4.2 collective-permute-start
  324.2 1.9 stack.40
  326.1 1.9 stack.39
  328.0 1.9 stack.41
  329.8 5.7 collective-permute-done
  335.5 5.2 collective-permute-start.1
  340.7 9.9 %convolution_convert_fusion.2 = bf16[1536,768]{1,0:T(8,128)(2,1)} fusion(bf16[2112,1536]{1,0:T(8,128)(2,1)} %copy-done.4, bf16[2112,384]{0,1:T(8,128)(2,1)} %bitcast.167, bf16[2112,384]{0,1:T(8,128)(2,1)} %bitcast.151), kind=kOutput, calls=%fused_computation.19 | convolution fusion | flops 4990500864 | bytes 12091392 | tf_op jit(solution)/shard_map/kd,ke->de/dot_general | solution.py:73
  350.6 1.9 stack.42
  355.1 4.2 all-to-all-start
  360.0 4.7 collective-permute-start.2
  366.7 19.8 %collective-permute-done.2 = bf16[64,3840]{1,0:T(8,128)(2,1)} collective-permute-done((bf16[64,3840]{1,0:T(8,128)(2,1)}, bf16[64,3840]{1,0:T(8,128)(2,1)}, u32[]{:S(2)}, u32[]{:S(2)}) %collective-permute-start.2) | collective-permute-done | bytes 491552 | tf_op jit(solution)/shard_map/ppermute | solution.py:170
  386.6 5.2 collective-permute-start.3
  395.4 6.0 collective-permute-done.3
  401.4 5.2 collective-permute-start.4
  406.6 1.9 constant_dynamic-update-slice_fusion.15
  408.5 2.1 fusion.102
  410.6 4.8 collective-permute-done.4
  415.3 5.2 collective-permute-start.5
  424.2 17.0 %collective-permute-done.5 = bf16[64,3840]{1,0:T(8,128)(2,1)S(1)} collective-permute-done((bf16[64,3840]{1,0:T(8,128)(2,1)}, bf16[64,3840]{1,0:T(8,128)(2,1)S(1)}, u32[]{:S(2)}, u32[]{:S(2)}) %collective-permute-start.5) | collective-permute-done | bytes 491552 | tf_op jit(solution)/shard_map/ppermute | solution.py:170
  441.2 5.1 collective-permute-start.6
  448.9 8.8 %collective-permute-done.6 = bf16[64,3840]{1,0:T(8,128)(2,1)S(1)} collective-permute-done((bf16[64,3840]{1,0:T(8,128)(2,1)S(1)}, bf16[64,3840]{1,0:T(8,128)(2,1)S(1)}, u32[]{:S(2)}, u32[]{:S(2)}) %collective-permute-start.6) | collective-permute-done | bytes 491552 | tf_op jit(solution)/shard_map/ppermute | solution.py:170
  459.4 1.9 constant_dynamic-update-slice_fusion.8
  461.3 1.9 constant_dynamic-update-slice_fusion.7
  465.0 1.9 constant_dynamic-update-slice_fusion.5
  470.3 2.0 fusion.35
  472.4 3.0 fusion.18
  475.3 2.9 fusion.20
  478.2 2.9 fusion.13
  481.3 2.1 convert_bitcast_fusion
  485.9 2.0 fusion.37
  487.9 7.3 %reduce-scatter.20.cloned.1.call-done = bf16[192,768]{1,0:T(8,128)(2,1)} async-done(((bf16[1536,768]{1,0:T(8,128)(2,1)}), bf16[192,768]{1,0:T(8,128)(2,1)}) %reduce-scatter.20.cloned.1.call-update) | async-done | bytes 294928 | tf_op jit(solution)/shard_map/reduce_scatter | solution.py:161
  495.2 2.1 reshape.193
  497.3 98.5 %reduce-scatter.22.cloned.1.call-done = f32[48,14]{1,0:T(8,128)} async-done(((f32[1536,14]{1,0:T(8,128)}), f32[48,14]{1,0:T(8,128)}) %reduce-scatter.22.cloned.1.call-update) | async-done | bytes 2704
  (197 shorter events, 57.5 us)
Async XLA Ops:
  7.2 1.6 copy-start
  7.2 46.9 %all-gather.10.cloned.1.call-start = ((), (), s32[]{:S(2)}) async-start(), calls=%async_computation.10 | async-start | bytes 1327104 | tf_op jit(solution)/shard_map/all_gather | solution.py:81
  7.9 98.9 %all-gather.8.cloned.1.call-start = ((), (), s32[]{:S(2)}) async-start(), calls=%async_computation.9 | async-start | bytes 2654208 | tf_op jit(solution)/shard_map/all_gather | solution.py:80
  8.7 145.2 %all-gather.6.cloned.1.call-start = ((), (), s32[]{:S(2)}) async-start(), calls=%async_computation.8 | async-start | bytes 7864320 | tf_op jit(solution)/shard_map/all_gather | solution.py:95
  8.8 2.2 copy-start.28
  8.8 2.6 copy-start.23
  8.8 2.6 copy-start.31
  11.4 3.1 copy-start.5
  11.4 3.4 copy-start.36
  11.4 3.9 copy-start.24
  11.4 3.9 copy-start.34
  13.2 183.8 %all-gather.12.cloned.1.call-start = ((), (), s32[]{:S(2)}) async-start(), calls=%async_computation.11 | async-start | bytes 1327104 | tf_op jit(solution)/shard_map/all_gather | solution.py:82
  13.8 213.9 %reduce-scatter.10.cloned.1.call-start = ((), (), s32[]{:S(2)}) async-start(), calls=%async_computation.12 | async-start | bytes 245760 | tf_op jit(solution)/shard_map/reduce_scatter | solution.py:115
  14.6 95.8 %copy-start.32 = (f32[16]{0:T(128)}, f32[16]{0:T(128)S(1)}, u32[]{:S(2)}) copy-start(f32[16]{0:T(128)S(1)} %broadcast_multiply_fusion.8) | copy-start | bytes 196
  22.3 134.9 %copy-start.8 = (bf16[64,1536]{1,0:T(8,128)(2,1)}, bf16[64,1536]{1,0:T(8,128)(2,1)S(1)}, u32[]{:S(2)}) copy-start(bf16[64,1536]{1,0:T(8,128)(2,1)S(1)} %all_gather.25) | copy-start | bytes 589828
  22.9 226.6 %copy-start.41 = (pred[2112]{0:T(1024)(128)(4,1)}, pred[2112]{0:T(1024)(128)(4,1)S(1)}, u32[]{:S(2)}) copy-start(pred[2112]{0:T(1024)(128)(4,1)S(1)} %concatenate.24) | copy-start | bytes 6340
  55.8 116.6 %copy-start.20 = (bf16[64,4,96]{2,1,0:T(4,128)(2,1)}, bf16[64,4,96]{2,1,0:T(4,128)(2,1)S(1)}, u32[]{:S(2)}) copy-start(bf16[64,4,96]{2,1,0:T(4,128)(2,1)S(1)} %reshape.183) | copy-start | bytes 147460
  153.8 3.5 copy-start.9
  157.2 5.5 copy-start.4
  176.0 73.5 %copy-start.46 = (f32[4,64]{1,0:T(4,128)}, f32[4,64]{1,0:T(4,128)S(1)}, u32[]{:S(2)}) copy-start(f32[4,64]{1,0:T(4,128)S(1)} %get-tuple-element.49) | copy-start | bytes 3076
  176.0 53.6 %copy-start.22 = (f32[1536]{0:T(1024)S(1)}, f32[1536]{0:T(1024)}, u32[]{:S(2)}) copy-start(f32[1536]{0:T(1024)} %param.26) | copy-start | bytes 18436
  176.0 53.6 %copy-start.35 = (f32[1536]{0:T(1024)S(1)}, f32[1536]{0:T(1024)}, u32[]{:S(2)}) copy-start(f32[1536]{0:T(1024)} %param.27) | copy-start | bytes 18436
  179.2 61.6 %copy-start.16 = (f32[64,384]{1,0:T(8,128)}, f32[64,384]{1,0:T(8,128)S(1)}, u32[]{:S(2)}) copy-start(f32[64,384]{1,0:T(8,128)S(1)} %reshape.185) | copy-start | bytes 294916
  199.5 66.1 %reduce-scatter.14.cloned.1.call-start = ((), (), s32[]{:S(2)}) async-start(), calls=%async_computation.14 | async-start | bytes 245760 | tf_op jit(solution)/shard_map/reduce_scatter | solution.py:126
  228.6 38.5 %copy-start.30 = (f32[16]{0:T(128)}, f32[16]{0:T(128)S(1)}, u32[]{:S(2)}) copy-start(f32[16]{0:T(128)S(1)} %broadcast_multiply_fusion.7) | copy-start | bytes 196
  229.6 37.5 %copy-start.33 = (f32[16]{0:T(128)}, f32[16]{0:T(128)S(1)}, u32[]{:S(2)}) copy-start(f32[16]{0:T(128)S(1)} %add_rsqrt_fusion.1) | copy-start | bytes 196
  236.1 4.7 copy-start.17
  236.1 4.7 copy-start.10
  249.3 16.3 %copy-start.13 = (bf16[16,1536]{1,0:T(8,128)(2,1)S(1)}, bf16[16,1536]{1,0:T(8,128)(2,1)}, u32[]{:S(2)}) copy-start(bf16[16,1536]{1,0:T(8,128)(2,1)} %reduce-scatter.10.cloned.1.call-done) | copy-start | bytes 147460
  249.3 115.4 %reduce-scatter.18.cloned.1.call-start = ((), (), s32[]{:S(2)}) async-start(), calls=%async_computation.16 | async-start | bytes 245760 | tf_op jit(solution)/shard_map/reduce_scatter | solution.py:156
  267.1 9.5 %copy-start.39 = (f32[16]{0:T(128)}, f32[16]{0:T(128)S(1)}, u32[]{:S(2)}) copy-start(f32[16]{0:T(128)S(1)} %get-tuple-element.57) | copy-start | bytes 196
  267.1 9.5 %copy-start.40 = (f32[16]{0:T(128)}, f32[16]{0:T(128)S(1)}, u32[]{:S(2)}) copy-start(f32[16]{0:T(128)S(1)} %get-tuple-element.58) | copy-start | bytes 196
  281.5 3.7 copy-start.37
  281.5 3.7 copy-start.43
  281.5 3.7 copy-start.14
  281.5 3.7 copy-start.25
  281.5 3.7 copy-start.42
  281.5 3.7 copy-start.44
  281.5 3.7 copy-start.45
  281.5 3.7 copy-start.47
  285.3 2.2 copy-start.21
  291.5 13.0 %copy-start.6 = (bf16[1536,384]{1,0:T(8,128)(2,1)S(1)}, bf16[1536,384]{1,0:T(8,128)(2,1)}, u32[]{:S(2)}) copy-start(bf16[1536,384]{1,0:T(8,128)(2,1)} %all-gather.10.cloned.1.call-done) | copy-start | bytes 3538948
  291.5 13.0 %copy-start.18 = (bf16[64,384]{1,0:T(8,128)(2,1)S(1)}, bf16[64,384]{1,0:T(8,128)(2,1)}, u32[]{:S(2)}) copy-start(bf16[64,384]{1,0:T(8,128)(2,1)} %convert_element_type.140) | copy-start | bytes 147460
  299.8 4.6 copy-start.7
  305.7 86.1 %reduce-scatter.12.cloned.1.call-start = ((), (), s32[]{:S(2)}) async-start(), calls=%async_computation.13 | async-start | bytes 245760 | tf_op jit(solution)/shard_map/reduce_scatter | solution.py:133
  309.8 168.5 %reduce-scatter.16.cloned.1.call-start = ((), (), s32[]{:S(2)}) async-start(), calls=%async_computation.15 | async-start | bytes 7864320 | tf_op jit(solution)/shard_map/reduce_scatter | solution.py:152
  320.0 15.5 %collective-permute-start = (bf16[64,3840]{1,0:T(8,128)(2,1)}, bf16[64,3840]{1,0:T(8,128)(2,1)}, u32[]{:S(2)}, u32[]{:S(2)}) collective-permute-start(bf16[64,3840]{1,0:T(8,128)(2,1)} %get-tuple-element.37), channel_id=1, source_target_pairs={{0,28},{4,0},{8,4},{12,8},{16,12},{20,16},{24,20},{28,24},{1,29},{... | collective-permute-start | bytes 1474568 | tf_op jit(solution)/shard_map/ppermute | solution.py:170
  329.8 22.6 %copy-start.27 = (f32[1536]{0:T(1024)S(1)}, f32[1536]{0:T(1024)}, u32[]{:S(2)}) copy-start(f32[1536]{0:T(1024)} %get-tuple-element.19) | copy-start | bytes 18436
  329.8 22.6 %copy-start.26 = (f32[1536]{0:T(1024)S(1)}, f32[1536]{0:T(1024)}, u32[]{:S(2)}) copy-start(f32[1536]{0:T(1024)} %get-tuple-element.25) | copy-start | bytes 18436
  335.5 24.5 %collective-permute-start.1 = (bf16[64,3840]{1,0:T(8,128)(2,1)}, bf16[64,3840]{1,0:T(8,128)(2,1)}, u32[]{:S(2)}, u32[]{:S(2)}) collective-permute-start(bf16[64,3840]{1,0:T(8,128)(2,1)} %collective-permute-done), channel_id=1, source_target_pairs={{0,28},{4,0},{8,4},{12,8},{16,12},{20,16},{24,20},{28,24},{1,29},{... | collective-permute-start | bytes 1474568 | tf_op jit(solution)/shard_map/ppermute | solution.py:170
  355.1 53.4 %all-to-all-start = ((bf16[8,4,64,192]{3,2,1,0:T(8,128)(2,1)}), bf16[8,4,64,192]{3,2,1,0:T(8,128)(2,1)}, u32[]{:S(2)}, u32[]{:S(2)}) async-start(bf16[8,4,64,192]{3,2,1,0:T(8,128)(2,1)} %copy.96), calls=%async_computation.5 | async-start | bytes 2097152 | tf_op jit(solution)/shard_map/all_to_all | solution.py:183
  359.4 135.9 %reduce-scatter.20.cloned.1.call-start = ((), (), s32[]{:S(2)}) async-start(), calls=%async_computation.17 | async-start | bytes 2654208 | tf_op jit(solution)/shard_map/reduce_scatter | solution.py:161
  360.0 235.9 %reduce-scatter.22.cloned.1.call-start = ((), (), s32[]{:S(2)}) async-start(), calls=%async_computation.18 | async-start | bytes 811008
  360.0 26.6 %collective-permute-start.2 = (bf16[64,3840]{1,0:T(8,128)(2,1)}, bf16[64,3840]{1,0:T(8,128)(2,1)}, u32[]{:S(2)}, u32[]{:S(2)}) collective-permute-start(bf16[64,3840]{1,0:T(8,128)(2,1)} %collective-permute-done.1), channel_id=1, source_target_pairs={{0,28},{4,0},{8,4},{12,8},{16,12},{20,16},{24,20},{28,24},{1,29},{... | collective-permute-start | bytes 1474568 | tf_op jit(solution)/shard_map/ppermute | solution.py:170
  386.6 14.8 %collective-permute-start.3 = (bf16[64,3840]{1,0:T(8,128)(2,1)}, bf16[64,3840]{1,0:T(8,128)(2,1)}, u32[]{:S(2)}, u32[]{:S(2)}) collective-permute-start(bf16[64,3840]{1,0:T(8,128)(2,1)} %collective-permute-done.2), channel_id=1, source_target_pairs={{0,28},{4,0},{8,4},{12,8},{16,12},{20,16},{24,20},{28,24},{1,29},{... | collective-permute-start | bytes 1474568 | tf_op jit(solution)/shard_map/ppermute | solution.py:170
  401.4 14.0 %collective-permute-start.4 = (bf16[64,3840]{1,0:T(8,128)(2,1)}, bf16[64,3840]{1,0:T(8,128)(2,1)}, u32[]{:S(2)}, u32[]{:S(2)}) collective-permute-start(bf16[64,3840]{1,0:T(8,128)(2,1)} %collective-permute-done.3), channel_id=1, source_target_pairs={{0,28},{4,0},{8,4},{12,8},{16,12},{20,16},{24,20},{28,24},{1,29},{... | collective-permute-start | bytes 1474568 | tf_op jit(solution)/shard_map/ppermute | solution.py:170
  408.5 50.1 %copy-start.11 = (bf16[64,1536]{1,0:T(8,128)(2,1)S(1)}, bf16[64,1536]{1,0:T(8,128)(2,1)}, u32[]{:S(2)}) copy-start(bf16[64,1536]{1,0:T(8,128)(2,1)} %get-tuple-element.55) | copy-start | bytes 589828
  408.5 50.1 %copy-start.19 = (bf16[64,384]{1,0:T(8,128)(2,1)S(1)}, bf16[64,384]{1,0:T(8,128)(2,1)}, u32[]{:S(2)}) copy-start(bf16[64,384]{1,0:T(8,128)(2,1)} %convert_element_type.140) | copy-start | bytes 147460
  415.3 25.8 %collective-permute-start.5 = (bf16[64,3840]{1,0:T(8,128)(2,1)}, bf16[64,3840]{1,0:T(8,128)(2,1)S(1)}, u32[]{:S(2)}, u32[]{:S(2)}) collective-permute-start(bf16[64,3840]{1,0:T(8,128)(2,1)} %collective-permute-done.4), channel_id=1, source_target_pairs={{0,28},{4,0},{8,4},{12,8},{16,12},{20,16},{24,20},{28,24},{1,29},{... | collective-permute-start | bytes 1474568 | tf_op jit(solution)/shard_map/ppermute | solution.py:170
  441.2 16.6 %collective-permute-start.6 = (bf16[64,3840]{1,0:T(8,128)(2,1)S(1)}, bf16[64,3840]{1,0:T(8,128)(2,1)S(1)}, u32[]{:S(2)}, u32[]{:S(2)}) collective-permute-start(bf16[64,3840]{1,0:T(8,128)(2,1)S(1)} %collective-permute-done.5), channel_id=1, source_target_pairs={{0,28},{4,0},{8,4},{12,8},{16,12},{20,16},{24,20},{28,24},{1,29},{... | collective-permute-start | bytes 1474568 | tf_op jit(solution)/shard_map/ppermute | solution.py:170
  478.2 3.0 copy-start.3
  481.2 2.2 copy-start.29
  483.4 2.5 copy-start.15
  483.4 118.5 %copy-start.1 = (bf16[8,1536]{1,0:T(8,128)(2,1)S(1)}, bf16[8,1536]{1,0:T(8,128)(2,1)}, u32[]{:S(2)}) copy-start(bf16[8,1536]{1,0:T(8,128)(2,1)} %param.21) | copy-start | bytes 73732
  (3 other events, 2.6 us)
Sparse Core Ops, SparseCore 0:
  10.2 43.8 all-gather.9
  56.2 50.4 all-gather.7
  108.9 44.8 all-gather.5
  155.9 41.1 all-gather.11
  199.9 18.4 reduce-scatter.9
  249.4 16.1 reduce-scatter.13
  305.8 19.7 reduce-scatter.17
  328.0 19.7 reduce-scatter.11
  350.4 58.8 reduce-scatter.15
  412.6 82.5 reduce-scatter.19
  500.4 95.4 reduce-scatter.21
